TPU v7x, 256 devices: a whole 4x4x8 slice. The times are simulated.
256 devices in a mesh: row: 8 (over y, core), box: 32 (over z, x).
Axes of the slice: x: 4, y: 4, z: 8, core: 2. Of those that a mesh axis runs over, the one named last changes fastest.
Arguments:
- solved: bfloat16 [2, 32768, 512], P(None, ('box', 'row')), may hold values from -6 to 6
- rhs: bfloat16 [8, 32768, 512], P('row', 'box'), may hold values from -6 to 6
- leaf_basis: bfloat16 [8, 3, 128, 256, 128], P('row', None, 'box'), may hold values from -0.375 to 0.375
- first_level: bfloat16 [8, 3, 32, 4, 4, 128, 128], P('row', None, 'box'), may hold values from -0.25 to 0.25
- second_level: bfloat16 [8, 3, 32, 32, 128, 128], P('row', None, 'box'), may hold values from -0.5 to 0.5
- third_level: bfloat16 [8, 3, 32, 32, 128, 128], P('row', None, 'box'), may hold values from -0.25 to 0.25
- fourth_level: bfloat16 [8, 3, 32, 2, 8, 128, 128], P('row', None, 'box'), may hold values from -0.1875 to 0.1875
- out_basis: bfloat16 [8, 3, 64, 512, 128], P('row', None, 'box'), may hold values from -0.5 to 0.5
Outputs:
- unknowns: bfloat16 [8, 32768, 512], P('row', 'box')
All inputs are finite; a program needn't handle non-finite values.
Results may differ from a plain program's by a relative error of at most 0.015.
Values may be sent and summed in bfloat16 or wider, within the bound.
A program may use at most 128 MiB of HBM per device.

v0:
```python
import jax
import jax.numpy as jnp
from jax import lax
from jax.sharding import PartitionSpec as P


def leaf_levels(inputs, basis, first_mats, second_mats):
    stack_size, row_count, columns = inputs.shape
    leaf_count = basis.shape[1]
    leaf_rows = basis.shape[2]
    rank_size = basis.shape[3]
    slot_count = second_mats.shape[1]
    leaf_coef = jnp.einsum(
        "jlpr,jlpn->jlrn",
        basis,
        inputs.reshape(stack_size, leaf_count, leaf_rows, columns),
        preferred_element_type=jnp.float32,
    ).astype(jnp.bfloat16)
    mid_coef = jnp.einsum(
        "jskrq,jkqn->jsrn", first_mats, leaf_coef, preferred_element_type=jnp.float32
    ).astype(jnp.bfloat16)
    slot_mats = second_mats.reshape(stack_size, 4, slot_count // 4, rank_size, rank_size)
    slot_coef = jnp.einsum(
        "jstrq,jsqn->jstrn", slot_mats, mid_coef, preferred_element_type=jnp.float32
    ).astype(jnp.bfloat16)
    return slot_coef.reshape(stack_size, slot_count, rank_size, columns)


def outer_levels(received, third_mats, fourth_mats, outer_basis):
    stack_size, slot_count, rank_size, columns = received.shape
    grouped = received.reshape(stack_size, slot_count // 4, 4, rank_size, columns)
    group_mats = third_mats.reshape(stack_size, slot_count // 4, 4, rank_size, rank_size)
    group_coef = jnp.einsum(
        "jgkrq,jgkqn->jgrn", group_mats, grouped, preferred_element_type=jnp.float32
    ).astype(jnp.bfloat16)
    half_coef = jnp.einsum(
        "jhgrq,jgqn->jhrn", fourth_mats, group_coef, preferred_element_type=jnp.float32
    ).astype(jnp.bfloat16)
    result = jnp.einsum(
        "jhpr,jhrn->jhpn", outer_basis, half_coef, preferred_element_type=jnp.float32
    )
    return result.reshape(stack_size, -1, columns)


def on_device(
    solved, rhs, leaf_basis, first_level, second_level, third_level, fourth_level, out_basis
):
    gathered = lax.all_gather(solved, "row", axis=1, tiled=True)
    basis = leaf_basis[0]
    first_mats = first_level[0, :, 0]
    second_mats = second_level[0, :, 0]
    third_mats = third_level[0, :, 0]
    fourth_mats = fourth_level[0, :, 0]
    outer_basis = out_basis[0]
    coefs = leaf_levels(gathered, basis[:2], first_mats[:2], second_mats[:2])
    received = lax.all_to_all(coefs, "box", split_axis=1, concat_axis=1, tiled=True)
    both = outer_levels(received, third_mats[:2], fourth_mats[:2], outer_basis[:2])
    residual = rhs[0].astype(jnp.float32) - both[0] - both[1]
    residual_b = residual.astype(jnp.bfloat16)
    diag_coefs = leaf_levels(residual_b[None], basis[2:], first_mats[2:], second_mats[2:])
    diag_received = lax.all_to_all(diag_coefs, "box", split_axis=1, concat_axis=1, tiled=True)
    correction = outer_levels(diag_received, third_mats[2:], fourth_mats[2:], outer_basis[2:])[0]
    return (residual + correction).astype(jnp.bfloat16)[None]


def solution(mesh):
    placed = (
        P(None, ("box", "row"), None),
        P("row", "box", None),
        P("row", None, "box", None, None),
        P("row", None, "box", None, None, None, None),
        P("row", None, "box", None, None, None),
        P("row", None, "box", None, None, None),
        P("row", None, "box", None, None, None, None),
        P("row", None, "box", None, None),
    )
    return jax.shard_map(
        on_device, mesh=mesh, in_specs=placed, out_specs=P("row", "box", None), check_vma=False
    )
```

profile of v0, /device:TPU:16, one launch (start us, length us, event | category | flops | bytes accessed | tf_op | source)
XLA Modules:
  0.0 403.4 jit_solution(10704803147370578556)
XLA Ops:
  6.5 0.0 all-gather.2.cloned.1.call-start
  6.5 0.7 all-gather.2.cloned.1.call-update
  7.3 0.0 slice-start
  7.3 31.6 %all-gather.2.cloned.1.call-done = bf16[2,1024,512]{2,1,0:T(8,128)(2,1)} async-done(((bf16[2,128,512]{2,1,0:T(8,128)(2,1)}), bf16[2,1024,512]{2,1,0:T(8,128)(2,1)}) %all-gather.2.cloned.1.call-update) | async-done | bytes 2097168 | tf_op jit(solution)/shard_map/all_gather | solution.py:48
  38.9 2.3 fusion.7
  41.2 6.9 %convolution_convert_fusion = bf16[2,4,512,8,128]{4,2,3,1,0:T(8,128)(2,1)} fusion(bf16[2,4,8,128,128]{4,3,2,1,0:T(8,128)(2,1)S(1)} %bitcast.169, bf16[2,4,128,512,1]{3,2,1,4,0:T(8,128)(2,1)S(1)} %fusion.7, bf16[1,3,1,4,4,128,128]{6,5,4,3,2,1,0:T(8,128)(2,1)} %param.11), kind=kOutput, calls=%fused_computation.2 | convolution fusion | flops 1615331328 | bytes 12582912 | tf_op jit(solution)/shard_map/jstrq,jsqn->jstrn/dot_general | solution.py:23
  48.1 7.6 %copy.9 = bf16[2,32,128,512]{2,3,0,1:T(8,128)(2,1)} copy(bf16[2,32,128,512]{2,3,1,0:T(8,128)(2,1)} %bitcast.165) | data formatting | bytes 16777216 | tf_op jit(solution)/shard_map/reshape | solution.py:26
  55.7 10.0 %all-to-all-start = ((bf16[2,32,128,512]{2,3,0,1:T(8,128)(2,1)}), bf16[2,32,128,512]{2,3,0,1:T(8,128)(2,1)}, u32[]{:S(2)}, u32[]{:S(2)}) async-start(bf16[2,32,128,512]{2,3,0,1:T(8,128)(2,1)} %copy.9), calls=%async_computation | async-start | bytes 16777216 | tf_op jit(solution)/shard_map/all_to_all | solution.py:56
  65.7 0.0 slice-start.2
  65.7 188.7 %all-to-all-done = bf16[2,32,128,512]{2,3,0,1:T(8,128)(2,1)} async-done(((bf16[2,32,128,512]{2,3,0,1:T(8,128)(2,1)}), bf16[2,32,128,512]{2,3,0,1:T(8,128)(2,1)}, u32[]{:S(2)}, u32[]{:S(2)}) %all-to-all-start) | async-done | bytes 8388640 | tf_op jit(solution)/shard_map/all_to_all | solution.py:56
  254.4 7.2 %bitcast_convert_fusion = bf16[2,8,512,128]{3,2,1,0:T(8,128)(2,1)} fusion(bf16[2,8,4,128,128]{4,3,2,1,0:T(8,128)(2,1)S(1)} %bitcast.172, bf16[2,8,4,128,512]{3,4,0,2,1:T(8,128)(2,1)} %bitcast.13), kind=kOutput, calls=%fused_computation.3 | convolution fusion | flops 1074790400 | bytes 12582912 | tf_op jit(solution)/shard_map/jgkrq,jgkqn->jgrn/dot_general | solution.py:33
  261.6 0.0 copy-done.3
  261.6 5.1 %convolution_bitcast_fusion = f32[2,2,512,512]{3,2,1,0:T(8,128)} fusion(bf16[2,8,512,128]{3,2,1,0:T(8,128)(2,1)} %bitcast_convert_fusion, bf16[1,3,1,2,8,128,128]{6,5,4,3,2,1,0:T(8,128)(2,1)} %param.14, bf16[1,3,2,512,128]{4,3,2,1,0:T(8,128)(2,1)S(1)} %copy-done.3), kind=kOutput, calls=%fused_computation.5 | convolution fusion | flops 805568512 | bytes 7864320 | tf_op jit(solution)/shard_map/jhpr,jhrn->jhpn/dot_general | solution.py:39
  266.7 2.8 fusion.51
  269.5 0.0 slice-start.1
  269.5 2.7 fusion.22
  272.2 0.0 slice-done.1
  272.2 4.8 %convolution_convert_fusion.1 = bf16[4,512,8,128]{3,1,2,0:T(8,128)(2,1)} fusion(bf16[4,8,128,128]{3,2,1,0:T(8,128)(2,1)S(1)} %bitcast.170, bf16[4,128,512,1]{1,2,0,3:T(8,128)(2,1)} %fusion.22, bf16[1,3,1,4,4,128,128]{6,5,4,3,2,1,0:T(8,128)(2,1)} %param.11), kind=kOutput, calls=%fused_computation.4 | convolution fusion | flops 807665664 | bytes 6291456 | tf_op jit(solution)/shard_map/jstrq,jsqn->jstrn/dot_general | solution.py:23
  277.0 13.5 %all-to-all-start.1 = ((bf16[1,32,128,512]{2,3,0,1:T(8,128)(2,1)}), bf16[1,32,128,512]{2,3,0,1:T(8,128)(2,1)}, u32[]{:S(2)}, u32[]{:S(2)}) async-start(bf16[1,32,128,512]{2,3,0,1:T(8,128)(2,1)} %bitcast.168), calls=%async_computation.1 | async-start | bytes 8388608 | tf_op jit(solution)/shard_map/all_to_all | solution.py:61
  290.5 0.0 slice-start.3
  290.5 94.1 %all-to-all-done.1 = bf16[1,32,128,512]{2,3,0,1:T(8,128)(2,1)} async-done(((bf16[1,32,128,512]{2,3,0,1:T(8,128)(2,1)}), bf16[1,32,128,512]{2,3,0,1:T(8,128)(2,1)}, u32[]{:S(2)}, u32[]{:S(2)}) %all-to-all-start.1) | async-done | bytes 4194336 | tf_op jit(solution)/shard_map/all_to_all | solution.py:61
  384.6 4.4 %fusion.9 = bf16[8,128,512,1]{1,2,0,3:T(8,128)(2,1)} fusion(bf16[8,4,128,512]{2,3,1,0:T(8,128)(2,1)} %bitcast.44, bf16[8,4,128,128]{3,2,1,0:T(8,128)(2,1)S(1)} %bitcast.173), kind=kOutput, calls=%fused_computation.18 | convolution fusion | flops 537395200 | bytes 6291456 | tf_op jit(solution)/shard_map/jgkrq,jgkqn->jgrn/dot_general | solution.py:33
  389.0 3.7 fusion.26
  392.7 3.8 fusion.4
  (10 shorter events, 0.0 us)
Async XLA Ops:
  6.5 32.4 %all-gather.2.cloned.1.call-start = ((), (), s32[]{:S(2)}) async-start(), calls=%async_computation.2 | async-start | bytes 2359296 | tf_op jit(solution)/shard_map/all_gather | solution.py:48
  7.3 33.9 %slice-start = ((bf16[1,3,1,32,128,128]{5,4,3,2,1,0:T(8,128)(2,1)}), bf16[1,2,1,32,128,128]{5,4,3,2,1,0:T(8,128)(2,1)S(1)}, s32[]{:S(2)}) async-start(bf16[1,3,1,32,128,128]{5,4,3,2,1,0:T(8,128)(2,1)} %param.12), calls=%async_computation.3 | async-start | bytes 4194304 | tf_op jit(solution)/shard_map/slice | solution.py:55
  55.7 198.7 %all-to-all-start = ((bf16[2,32,128,512]{2,3,0,1:T(8,128)(2,1)}), bf16[2,32,128,512]{2,3,0,1:T(8,128)(2,1)}, u32[]{:S(2)}, u32[]{:S(2)}) async-start(bf16[2,32,128,512]{2,3,0,1:T(8,128)(2,1)} %copy.9), calls=%async_computation | async-start | bytes 16777216 | tf_op jit(solution)/shard_map/all_to_all | solution.py:56
  65.7 188.8 %slice-start.2 = ((bf16[1,3,1,32,128,128]{5,4,3,2,1,0:T(8,128)(2,1)}), bf16[1,2,1,32,128,128]{5,4,3,2,1,0:T(8,128)(2,1)S(1)}, s32[]{:S(2)}) async-start(bf16[1,3,1,32,128,128]{5,4,3,2,1,0:T(8,128)(2,1)} %param.13), calls=%async_computation.5 | async-start | bytes 4194304 | tf_op jit(solution)/shard_map/slice | solution.py:57
  254.4 7.2 %copy-start.3 = (bf16[1,3,2,512,128]{4,3,2,1,0:T(8,128)(2,1)S(1)}, bf16[1,3,2,512,128]{4,3,2,1,0:T(8,128)(2,1)}, u32[]{:S(2)}) copy-start(bf16[1,3,2,512,128]{4,3,2,1,0:T(8,128)(2,1)} %param.15) | copy-start | bytes 2359300
  266.7 2.8 copy-start.1
  269.5 2.7 copy-start
  269.5 2.7 slice-start.1
  277.0 107.6 %all-to-all-start.1 = ((bf16[1,32,128,512]{2,3,0,1:T(8,128)(2,1)}), bf16[1,32,128,512]{2,3,0,1:T(8,128)(2,1)}, u32[]{:S(2)}, u32[]{:S(2)}) async-start(bf16[1,32,128,512]{2,3,0,1:T(8,128)(2,1)} %bitcast.168), calls=%async_computation.1 | async-start | bytes 8388608 | tf_op jit(solution)/shard_map/all_to_all | solution.py:61
  290.5 94.1 %slice-start.3 = ((bf16[1,3,1,32,128,128]{5,4,3,2,1,0:T(8,128)(2,1)}), bf16[1,1,1,32,128,128]{5,4,3,2,1,0:T(8,128)(2,1)S(1)}, s32[]{:S(2)}) async-start(bf16[1,3,1,32,128,128]{5,4,3,2,1,0:T(8,128)(2,1)} %param.13), calls=%async_computation.6 | async-start | bytes 2097152 | tf_op jit(solution)/shard_map/slice | solution.py:62
  389.0 3.7 copy-start.2
Sparse Core Ops, SparseCore 0:
  9.2 29.6 all-gather.1
where the time goes:
time: 408 us; the launch traced here: 403 us
  waiting for transfers between devices  315 us (77%)
  matrix products  37 us (9%)
  starting transfers between devices  23.5 us (6%)
  between operations  13.5 us (3%)
  local copies, waits for them, and re-layouts  10.4 us (3%)
    all_to_all x1, waiting for transfers between devices, on_device(): lax.all_to_all(coefs, 'box', split_axis=1, concat_axis=1, tiled=True)  189 us
    all_to_all x1, waiting for transfers between devices, on_device(): lax.all_to_all(diag_coefs, 'box', split_axis=1, concat_axis=1, tiled=True)  94.1 us
    all_gather x1, waiting for transfers between devices, on_device(): gathered = lax.all_gather(solved, 'row', axis=1, tiled=True)  31.6 us
    all_to_all x1, starting transfers between devices, on_device(): lax.all_to_all(diag_coefs, 'box', split_axis=1, concat_axis=1, tiled=True)  13.5 us
    dot_general x2, matrix products, leaf_levels(): jnp.einsum('jstrq,jsqn->jstrn', slot_mats, mid_coef, preferred_element_ty...  11.7 us
    dot_general x2, matrix products, outer_levels(): jnp.einsum('jgkrq,jgkqn->jgrn', group_mats, grouped, preferred_element_ty...  11.6 us
    all_to_all x1, starting transfers between devices, on_device(): lax.all_to_all(coefs, 'box', split_axis=1, concat_axis=1, tiled=True)  9.95 us
    dot_general x2, matrix products, outer_levels(): jnp.einsum('jhpr,jhrn->jhpn', outer_basis, half_coef, preferred_element_t...  8.81 us
  transfers between devices with their start and end apart: 3, of which 3 were waited for; matrix products, arithmetic and copies ran while one was open for 0% of the time, Pallas kernels for 0%

commit v1 on v0

v1 whole, which is shorter than its diff:
```python
import jax
import jax.numpy as jnp
from jax import lax
from jax.sharding import PartitionSpec as P

F32 = jnp.float32
BF16 = jnp.bfloat16
NX = 4


def dot(spec, a, b):
    return jnp.einsum(spec, a, b, preferred_element_type=F32)


def on_device(n_box, solved, rhs, leaf_basis, first_level, second_level, third_level, fourth_level, out_basis):
    nz = n_box // NX
    along_z = [[z * NX + x for z in range(nz)] for x in range(NX)]
    along_x = [[z * NX + x for x in range(NX)] for z in range(nz)]
    gathered = lax.all_gather(solved, "row", axis=1, tiled=True)
    basis, first, second = leaf_basis[0], first_level[0, :, 0], second_level[0, :, 0]
    third, fourth, outer = third_level[0, :, 0], fourth_level[0, :, 0], out_basis[0]
    rank = basis.shape[-1]
    third = third.reshape(3, nz, NX, rank, rank)
    outer_w = dot("jhqab,jqkbc->kjhaqc", fourth, third).astype(BF16)
    outer_w = lax.all_to_all(outer_w, "box", 0, 0, axis_index_groups=along_x, tiled=True)
    second = second.reshape(3, nz, NX, rank, rank)
    second = lax.all_to_all(second, "box", 1, 1, axis_index_groups=along_z, tiled=True)
    full = dot("xjhaqc,jqxcd->jxhaqd", outer_w, second).astype(BF16)
    full = full.reshape(3, NX, 2 * rank, nz * rank)

    def middle(js, inputs):
        n = inputs.shape[0]
        columns = inputs.shape[-1]
        leaf = dot("jlpr,jlpn->jlrn", basis[js], inputs.reshape(n, 4, -1, columns)).astype(BF16)
        mid = dot("jskrq,jkqn->jsrn", first[js], leaf).astype(BF16)
        mid = jnp.repeat(mid, nz // 4, axis=1)
        mid = lax.all_to_all(mid, "box", 1, 1, axis_index_groups=along_z, tiled=True)
        part = dot("jxab,jbn->jxan", full[js], mid.reshape(n, nz * rank, columns)).astype(BF16)
        part = lax.all_to_all(part, "box", 1, 1, axis_index_groups=along_x, tiled=True)
        half = part.astype(F32).sum(1).astype(BF16).reshape(n, 2, rank, columns)
        return dot("jhpr,jhrn->jhpn", outer[js], half).reshape(n, -1, columns)

    both = middle(slice(0, 2), gathered)
    residual = rhs[0].astype(F32) - both[0] - both[1]
    correction = middle(slice(2, 3), residual.astype(BF16)[None])[0]
    return (residual + correction).astype(BF16)[None]


def solution(mesh):
    placed = (
        P(None, ("box", "row"), None),
        P("row", "box", None),
        P("row", None, "box", None, None),
        P("row", None, "box", None, None, None, None),
        P("row", None, "box", None, None, None),
        P("row", None, "box", None, None, None),
        P("row", None, "box", None, None, None, None),
        P("row", None, "box", None, None),
    )

    def run(*args):
        return on_device(mesh.shape["box"], *args)

    return jax.shard_map(run, mesh=mesh, in_specs=placed, out_specs=P("row", "box", None), check_vma=False)
```

time: 408 us -> 357 us (0.88)
  waiting for transfers between devices: 315 us -> 209 us
  local copies, waits for them, and re-layouts: 10.4 us -> 57 us
  blocking collectives: 0 us -> 18 us
  matrix products: 37 us -> 24.6 us
  starting transfers between devices: 23.5 us -> 28.2 us
    all_to_all x2 -> x5, waiting for transfers between devices: 283 us -> 180 us  [the longest x1 67.7 us: on_device(): lax.all_to_all(outer_w, 'box', 0, 0, axis_index_groups=along_x, tiled=True)]
    all_to_all x0 -> x1, blocking collectives: none -> 18 us  [middle(): lax.all_to_all(part, 'box', 1, 1, axis_index_groups=along_x, tiled=True)]
    slice x9 -> x7, local copies, waits for them, and re-layouts: 2.78 us -> 20.2 us  [the longest x6 17.7 us: middle(): full[js]]
    convert_element_type x0 -> x5, local copies, waits for them, and re-layouts: none -> 12.5 us  [the longest x1 8.61 us: on_device(): outer_w = dot('jhqab,jqkbc->kjhaqc', fourth, third).astype(BF16)]
    dot_general x8, matrix products: 37 us -> 24.6 us  [dot(): return jnp.einsum(spec, a, b, preferred_element_type=F32)]
    another operation x0 -> x2, local copies, waits for them, and re-layouts: none -> 8.11 us
    reshape x1 -> x0, local copies, waits for them, and re-layouts: 7.61 us -> none  [leaf_levels(): return slot_coef.reshape(stack_size, slot_count, rank_size, columns)]
    unnamed x8 -> x18, local copies, waits for them, and re-layouts: 0.02 us -> 5.83 us
  transfers between devices with their start and end apart: 3 -> 6, of which waited for: 3 -> 6; matrix products, arithmetic and copies ran while one was open for 0% -> 10% of each run, Pallas kernels for 0% -> 0%
where the time goes in v1:
time: 357 us; the launch traced here: 356 us
  waiting for transfers between devices  209 us (59%)
  local copies, waits for them, and re-layouts  57 us (16%)
  starting transfers between devices  28.2 us (8%)
  matrix products  24.6 us (7%)
  blocking collectives  18 us (5%)
  between operations  13.5 us (4%)
  other arithmetic  5.76 us (2%)
    all_to_all x1, waiting for transfers between devices, on_device(): lax.all_to_all(outer_w, 'box', 0, 0, axis_index_groups=along_x, tiled=True)  67.7 us
    all_to_all x2, waiting for transfers between devices, middle(): lax.all_to_all(mid, 'box', 1, 1, axis_index_groups=along_z, tiled=True)  46.4 us
    all_to_all x1, waiting for transfers between devices, on_device(): lax.all_to_all(second, 'box', 1, 1, axis_index_groups=along_z, tiled=True)  40.5 us
    all_gather x1, waiting for transfers between devices, on_device(): gathered = lax.all_gather(solved, 'row', axis=1, tiled=True)  28.5 us
    all_to_all x1, waiting for transfers between devices, middle(): lax.all_to_all(part, 'box', 1, 1, axis_index_groups=along_x, tiled=True)  25.1 us
    dot_general x8, matrix products, dot(): return jnp.einsum(spec, a, b, preferred_element_type=F32)  24.6 us
    all_to_all x1, blocking collectives, middle(): lax.all_to_all(part, 'box', 1, 1, axis_index_groups=along_x, tiled=True)  18 us
    slice x6, local copies, waits for them, and re-layouts, middle(): full[js]  17.7 us
  transfers between devices with their start and end apart: 6, of which 6 were waited for; matrix products, arithmetic and copies ran while one was open for 10% of the time, Pallas kernels for 0%

profile of v1, /device:TPU:16, one launch (start us, length us, event | category | flops | bytes accessed | tf_op | source)
XLA Modules:
  0.0 356.0 jit_solution(732487623637199776)
XLA Ops:
  7.9 6.4 %convert_bitcast_fusion.1 = bf16[4,3,2,128,8,128]{3,5,2,4,0,1:T(8,128)(2,1)} fusion(bf16[3,8,4,128,128,1]{4,3,2,1,0,5:T(8,128)(2,1)} %bitcast.119, bf16[1,3,1,2,8,128,128]{6,5,4,3,2,1,0:T(8,128)(2,1)S(1)} %copy-done), kind=kOutput, calls=%fused_computation.3 | convolution fusion | flops 808452096 | bytes 11010048 | tf_op jit(solution)/shard_map/jhqab,jqkbc->kjhaqc/dot_general | solution.py:12
  14.3 8.6 %copy.20 = bf16[4,3,2,128,8,128]{5,3,2,4,1,0:T(8,128)(2,1)} copy(bf16[4,3,2,128,8,128]{3,5,2,4,0,1:T(8,128)(2,1)} %convert_bitcast_fusion.1) | data formatting | bytes 12582912 | tf_op jit(solution)/shard_map/convert_element_type | solution.py:24
  23.0 5.3 %all-to-all-start = ((bf16[4,3,2,128,8,128]{5,3,2,4,1,0:T(8,128)(2,1)}), bf16[4,3,2,128,8,128]{5,3,2,4,1,0:T(8,128)(2,1)}, u32[]{:S(2)}, u32[]{:S(2)}) async-start(bf16[4,3,2,128,8,128]{5,3,2,4,1,0:T(8,128)(2,1)} %copy.20), calls=%async_computation | async-start | bytes 12582912 | tf_op jit(solution)/shard_map/all_to_all | solution.py:25
  28.2 4.0 %copy.21 = bf16[3,8,4,128,128]{4,3,2,0,1:T(8,128)(2,1)} copy(bf16[3,8,4,128,128]{4,3,2,1,0:T(8,128)(2,1)} %bitcast.121) | data formatting | bytes 6291456 | tf_op jit(solution)/shard_map/reshape;squeeze | solution.py:26
  32.2 67.7 %all-to-all-done = bf16[4,3,2,128,8,128]{5,3,2,4,1,0:T(8,128)(2,1)} async-done(((bf16[4,3,2,128,8,128]{5,3,2,4,1,0:T(8,128)(2,1)}), bf16[4,3,2,128,8,128]{5,3,2,4,1,0:T(8,128)(2,1)}, u32[]{:S(2)}, u32[]{:S(2)}) %all-to-all-start) | async-done | bytes 6291488 | tf_op jit(solution)/shard_map/all_to_all | solution.py:25
  99.8 8.5 %all-to-all-start.1 = ((bf16[3,8,4,128,128]{4,3,2,0,1:T(8,128)(2,1)}), bf16[3,8,4,128,128]{4,3,2,0,1:T(8,128)(2,1)}, u32[]{:S(2)}, u32[]{:S(2)}) async-start(bf16[3,8,4,128,128]{4,3,2,0,1:T(8,128)(2,1)} %copy.21), calls=%async_computation.1 | async-start | bytes 6291456 | tf_op jit(solution)/shard_map/all_to_all | solution.py:27
  109.0 28.5 %all-gather.2.cloned.1.call-done = bf16[2,1024,512]{2,1,0:T(8,128)(2,1)} async-done(((bf16[2,128,512]{2,1,0:T(8,128)(2,1)}), bf16[2,1024,512]{2,1,0:T(8,128)(2,1)}) %all-gather.2.cloned.1.call-update) | async-done | bytes 2097168 | tf_op jit(solution)/shard_map/all_gather | solution.py:19
  140.8 40.5 %all-to-all-done.1 = bf16[3,8,4,128,128]{4,3,2,0,1:T(8,128)(2,1)} async-done(((bf16[3,8,4,128,128]{4,3,2,0,1:T(8,128)(2,1)}), bf16[3,8,4,128,128]{4,3,2,0,1:T(8,128)(2,1)}, u32[]{:S(2)}, u32[]{:S(2)}) %all-to-all-start.1) | async-done | bytes 3145760 | tf_op jit(solution)/shard_map/all_to_all | solution.py:27
  182.9 4.5 %all-to-all-start.2 = ((bf16[2,8,128,512]{3,2,0,1:T(8,128)(2,1)}), bf16[2,8,128,512]{3,2,0,1:T(8,128)(2,1)}, u32[]{:S(2)}, u32[]{:S(2)}) async-start(bf16[2,8,128,512]{3,2,0,1:T(8,128)(2,1)} %bitcast.118), calls=%async_computation.2 | async-start | bytes 4194304 | tf_op jit(solution)/shard_map/all_to_all | solution.py:37
  187.5 5.5 %convert_bitcast_fusion = bf16[3,4,2,128,8,128]{5,3,2,4,1,0:T(8,128)(2,1)S(1)} fusion(bf16[4,3,2,128,8,128]{5,3,2,4,1,0:T(8,128)(2,1)} %all-to-all-done, bf16[3,8,4,128,128]{4,3,2,0,1:T(8,128)(2,1)} %all-to-all-done.1), kind=kOutput, calls=%fused_computation.2 | convolution fusion | flops 808452096 | bytes 15728640 | tf_op jit(solution)/shard_map/xjhaqc,jqxcd->jxhaqd/dot_general | solution.py:12
  195.6 5.7 %copy.24 = bf16[2,4,2,128,8,128]{5,4,3,2,1,0:T(8,128)(2,1)} copy(bf16[2,4,2,128,8,128]{5,3,2,4,1,0:T(8,128)(2,1)S(1)} %slice.62) | data formatting | bytes 8388608 | tf_op jit(solution)/shard_map/slice | solution.py:38
  201.3 7.3 %slice.49 = bf16[2,4,256,1024]{3,2,1,0:T(8,128)(2,1)} reshape(bf16[2,4,2,128,8,128]{5,4,3,2,1,0:T(8,128)(2,1)} %copy.24) | data formatting | bytes 8388608 | tf_op jit(solution)/shard_map/slice | solution.py:38
  208.6 26.9 %all-to-all-done.2 = bf16[2,8,128,512]{3,2,0,1:T(8,128)(2,1)} async-done(((bf16[2,8,128,512]{3,2,0,1:T(8,128)(2,1)}), bf16[2,8,128,512]{3,2,0,1:T(8,128)(2,1)}, u32[]{:S(2)}, u32[]{:S(2)}) %all-to-all-start.2) | async-done | bytes 2097184 | tf_op jit(solution)/shard_map/all_to_all | solution.py:37
  242.2 4.6 %all-to-all-start.3 = ((bf16[2,4,256,512]{3,2,0,1:T(8,128)(2,1)}), bf16[2,4,256,512]{3,2,0,1:T(8,128)(2,1)}, u32[]{:S(2)}, u32[]{:S(2)}) async-start(bf16[2,4,256,512]{3,2,0,1:T(8,128)(2,1)} %copy.30), calls=%async_computation.3 | async-start | bytes 4194304 | tf_op jit(solution)/shard_map/all_to_all | solution.py:39
  248.4 25.1 %all-to-all-done.3 = bf16[2,4,256,512]{3,2,0,1:T(8,128)(2,1)} async-done(((bf16[2,4,256,512]{3,2,0,1:T(8,128)(2,1)}), bf16[2,4,256,512]{3,2,0,1:T(8,128)(2,1)}, u32[]{:S(2)}, u32[]{:S(2)}) %all-to-all-start.3) | async-done | bytes 2097184 | tf_op jit(solution)/shard_map/all_to_all | solution.py:39
  278.8 2.9 copy.34
  281.7 2.9 copy.33
  284.6 3.7 %fusion.13 = bf16[4,128,512]{1,2,0:T(8,128)(2,1)S(1)} fusion(f32[4,256,512]{1,2,0:T(8,128)} %copy.34, f32[4,256,512]{1,2,0:T(8,128)} %copy.32, f32[4,256,512]{1,2,0:T(8,128)} %copy.33, bf16[1,3,1,4,4,128,128]{6,5,4,3,2,1,0:T(8,128)(2,1)} %param.11, bf16[1,3,4,256,128]{4,3,2,1,0:T(8,128)(2,1)} %param.10), kind=kOutput, calls=%fused_computation.24 | convolution fusion | flops 404750336 | bytes 7602176 | tf_op jit(solution)/shard_map/jskrq,jkqn->jsrn/dot_general | solution.py:12
  289.7 5.3 %all-to-all-start.4 = ((bf16[1,8,128,512]{3,2,0,1:T(8,128)(2,1)}), bf16[1,8,128,512]{3,2,0,1:T(8,128)(2,1)S(1)}, u32[]{:S(2)}, u32[]{:S(2)}) async-start(bf16[1,8,128,512]{3,2,0,1:T(8,128)(2,1)} %bitcast.35), calls=%async_computation.4 | async-start | bytes 2097152 | tf_op jit(solution)/shard_map/all_to_all | solution.py:37
  299.4 4.2 %reshape.86 = bf16[4,256,1024]{2,1,0:T(8,128)(2,1)} reshape(bf16[1,4,2,128,8,128]{5,4,3,2,1,0:T(8,128)(2,1)} %copy.31) | data formatting | bytes 4194304 | tf_op jit(solution)/shard_map/reshape.28
  303.5 19.5 %all-to-all-done.4 = bf16[1,8,128,512]{3,2,0,1:T(8,128)(2,1)S(1)} async-done(((bf16[1,8,128,512]{3,2,0,1:T(8,128)(2,1)}), bf16[1,8,128,512]{3,2,0,1:T(8,128)(2,1)S(1)}, u32[]{:S(2)}, u32[]{:S(2)}) %all-to-all-start.4) | async-done | bytes 1048608 | tf_op jit(solution)/shard_map/all_to_all | solution.py:37
  323.1 2.8 fusion.9
  325.9 18.0 %all_to_all.30 = bf16[1,4,256,512]{3,2,0,1:T(8,128)(2,1)S(1)} all-to-all(bf16[1,4,256,512]{3,2,0,1:T(8,128)(2,1)S(1)} %fusion.9), channel_id=1, replica_groups={{0,1,2,3},{4,5,6,7},{8,9,10,11},{12,13,14,15},{16,17,18,19},{20,21,22,2..., dimensions={1} | all-to-all | bytes 2097152 | tf_op jit(solution)/shard_map/all_to_all | solution.py:39
  345.7 3.4 fusion.6
  (38 shorter events, 30.7 us)
Async XLA Ops:
  6.5 1.4 copy-start
  23.0 76.9 %all-to-all-start = ((bf16[4,3,2,128,8,128]{5,3,2,4,1,0:T(8,128)(2,1)}), bf16[4,3,2,128,8,128]{5,3,2,4,1,0:T(8,128)(2,1)}, u32[]{:S(2)}, u32[]{:S(2)}) async-start(bf16[4,3,2,128,8,128]{5,3,2,4,1,0:T(8,128)(2,1)} %copy.20), calls=%async_computation | async-start | bytes 12582912 | tf_op jit(solution)/shard_map/all_to_all | solution.py:25
  32.2 105.4 %copy-start.7 = (bf16[1,3,1,4,4,128,128]{6,5,4,3,2,1,0:T(8,128)(2,1)S(1)}, bf16[1,3,1,4,4,128,128]{6,5,4,3,2,1,0:T(8,128)(2,1)}, u32[]{:S(2)}) copy-start(bf16[1,3,1,4,4,128,128]{6,5,4,3,2,1,0:T(8,128)(2,1)} %param.11) | copy-start | bytes 4718596
  32.2 105.4 %copy-start.8 = (bf16[1,3,4,256,128]{4,3,2,1,0:T(8,128)(2,1)S(1)}, bf16[1,3,4,256,128]{4,3,2,1,0:T(8,128)(2,1)}, u32[]{:S(2)}) copy-start(bf16[1,3,4,256,128]{4,3,2,1,0:T(8,128)(2,1)} %param.10) | copy-start | bytes 2359300
  99.8 81.5 %all-to-all-start.1 = ((bf16[3,8,4,128,128]{4,3,2,0,1:T(8,128)(2,1)}), bf16[3,8,4,128,128]{4,3,2,0,1:T(8,128)(2,1)}, u32[]{:S(2)}, u32[]{:S(2)}) async-start(bf16[3,8,4,128,128]{4,3,2,0,1:T(8,128)(2,1)} %copy.21), calls=%async_computation.1 | async-start | bytes 6291456 | tf_op jit(solution)/shard_map/all_to_all | solution.py:27
  108.3 29.3 %all-gather.2.cloned.1.call-start = ((), (), s32[]{:S(2)}) async-start(), calls=%async_computation.6 | async-start | bytes 2359296 | tf_op jit(solution)/shard_map/all_gather | solution.py:19
  182.9 52.6 %all-to-all-start.2 = ((bf16[2,8,128,512]{3,2,0,1:T(8,128)(2,1)}), bf16[2,8,128,512]{3,2,0,1:T(8,128)(2,1)}, u32[]{:S(2)}, u32[]{:S(2)}) async-start(bf16[2,8,128,512]{3,2,0,1:T(8,128)(2,1)} %bitcast.118), calls=%async_computation.2 | async-start | bytes 4194304 | tf_op jit(solution)/shard_map/all_to_all | solution.py:37
  193.0 2.7 copy-start.2
  235.5 2.8 copy-start.4
  242.2 4.6 %copy-start.5 = (bf16[1,1024,512]{2,1,0:T(8,128)(2,1)S(1)}, bf16[1,1024,512]{2,1,0:T(8,128)(2,1)}, u32[]{:S(2)}) copy-start(bf16[1,1024,512]{2,1,0:T(8,128)(2,1)} %param.9) | copy-start | bytes 3145732
  242.2 31.3 %all-to-all-start.3 = ((bf16[2,4,256,512]{3,2,0,1:T(8,128)(2,1)}), bf16[2,4,256,512]{3,2,0,1:T(8,128)(2,1)}, u32[]{:S(2)}, u32[]{:S(2)}) async-start(bf16[2,4,256,512]{3,2,0,1:T(8,128)(2,1)} %copy.30), calls=%async_computation.3 | async-start | bytes 4194304 | tf_op jit(solution)/shard_map/all_to_all | solution.py:39
  248.4 27.2 %copy-start.6 = (bf16[1,3,2,512,128]{4,3,2,1,0:T(8,128)(2,1)S(1)}, bf16[1,3,2,512,128]{4,3,2,1,0:T(8,128)(2,1)}, u32[]{:S(2)}) copy-start(bf16[1,3,2,512,128]{4,3,2,1,0:T(8,128)(2,1)} %param.15) | copy-start | bytes 2359300
  289.7 33.4 %all-to-all-start.4 = ((bf16[1,8,128,512]{3,2,0,1:T(8,128)(2,1)}), bf16[1,8,128,512]{3,2,0,1:T(8,128)(2,1)S(1)}, u32[]{:S(2)}, u32[]{:S(2)}) async-start(bf16[1,8,128,512]{3,2,0,1:T(8,128)(2,1)} %bitcast.35), calls=%async_computation.4 | async-start | bytes 2097152 | tf_op jit(solution)/shard_map/all_to_all | solution.py:37
  295.0 1.6 slice-start
  344.1 1.6 copy-start.3
  345.7 3.4 copy-start.1
Sparse Core Ops, SparseCore 0:
  110.9 26.5 all-gather.1

commit v2 on v1

v2 whole, which is shorter than its diff:
```python
import functools

import jax
import jax.numpy as jnp
from jax import lax
from jax.experimental import pallas as pl
from jax.experimental.pallas import tpu as pltpu
from jax.sharding import PartitionSpec as P

F32 = jnp.float32
BF16 = jnp.bfloat16
MESH = pl.DeviceIdType.MESH
NX, NZ, NY = 4, 8, 4
X_DISTS = (2, 1, 3)
Z_DISTS = (4, 3, 5, 2, 6, 1, 7)
RANK, COLS = 128, 512


def dot(a, b):
    return jnp.dot(a, b, preferred_element_type=F32)


def kernel(
    solved, rhs, leaf, first, second, third, fourth, outer, out,
    gath, leaf_v, leaf_t, first_v, third_v, fourth_v, outer_v, rhs_v,
    w_send, w_recv, sec, full, leaf_c, m_send, m_recv, p_send, p_recv, half, res, res_b,
    load_sem, own_sem, ag_s, ag_r, w_s, w_r, sec_s, sec_r, m_s, m_r, p_s, p_r,
):
    row, box = lax.axis_index("row"), lax.axis_index("box")
    y, core = row // 2, row % 2
    z, x = box // NX, box % NX

    def at_z(plane):
        return (row, plane * NX + x)

    def at_x(col):
        return (row, z * NX + col)

    def at_y(chip):
        return (chip * 2 + core, box)

    partner = (y * 2 + 1 - core, box)
    other_z = z + 1 - 2 * (z % 2)

    def remote(src, dst, send, recv, device):
        return pltpu.make_async_remote_copy(
            src_ref=src, dst_ref=dst, send_sem=send, recv_sem=recv, device_id=device, device_id_type=MESH
        )

    barrier = pltpu.get_barrier_semaphore()
    peers = [partner] + [at_y((y + i) % NY) for i in range(1, NY)]
    peers += [at_x((x + i) % NX) for i in range(1, NX)] + [at_z((z + i) % NZ) for i in range(1, NZ)]
    for peer in peers:
        pl.semaphore_signal(barrier, inc=1, device_id=peer, device_id_type=MESH)

    loads = [
        (third.at[0, 0, 0], third_v.at[0]),
        (fourth.at[0, 0, 0], fourth_v.at[0]),
        (third.at[0, 1, 0], third_v.at[1]),
        (fourth.at[0, 1, 0], fourth_v.at[1]),
        (third.at[0, 2, 0], third_v.at[2]),
        (fourth.at[0, 2, 0], fourth_v.at[2]),
        (leaf.at[0], leaf_v),
        (first.at[0, :, 0], first_v),
        (solved, gath.at[:, row]),
        (outer.at[0], outer_v),
        (rhs.at[0], rhs_v),
        (second.at[0, 0, 0, pl.ds(z * NX, NX)], sec.at[0, z]),
        (second.at[0, 1, 0, pl.ds(z * NX, NX)], sec.at[1, z]),
        (second.at[0, 2, 0, pl.ds(z * NX, NX)], sec.at[2, z]),
    ]
    loads = [pltpu.make_async_copy(src, dst, load_sem.at[i]) for i, (src, dst) in enumerate(loads)]
    for copy in loads:
        copy.start()
    pl.semaphore_wait(barrier, len(peers))

    sends = []

    def start(copy):
        copy.start()
        sends.append(copy)

    for n, i in enumerate((1, 3, 2)):
        start(remote(solved, gath.at[:, row], ag_s.at[n], ag_r.at[row], at_y((y + i) % NY)))
    start(remote(solved, gath.at[:, row], ag_s.at[3], ag_r.at[row], partner))

    def send_second(j):
        for n, i in enumerate(Z_DISTS):
            plane = (z + i) % NZ
            start(remote(second.at[0, j, 0, pl.ds(plane * NX, NX)], sec.at[j, z], sec_s.at[j, n], sec_r.at[j, n], at_z(plane)))

    def wait_second(j):
        for n, i in enumerate(Z_DISTS):
            plane = (z - i + NZ) % NZ
            remote(sec.at[j, plane], sec.at[j, plane], sec_s.at[j, n], sec_r.at[j, n], at_z(plane)).wait_recv()
        loads[11 + j].wait()

    def outer_weights(j):
        loads[2 * j].wait()
        loads[2 * j + 1].wait()

        @pl.loop(0, NZ)
        def _(q):
            a = fourth_v[j, :, q].reshape(2 * RANK, RANK)
            b = jnp.concatenate([third_v[j, q * NX + k] for k in range(NX)], axis=1)
            o = dot(a, b).astype(BF16)
            for k in range(NX):
                w_send[j, k, q] = o[:, k * RANK : (k + 1) * RANK]

        for n, i in enumerate(X_DISTS):
            col = (x + i) % NX
            start(remote(w_send.at[j, col], w_recv.at[j, x], w_s.at[j, n], w_r.at[j, n], at_x(col)))
        pltpu.make_async_copy(w_send.at[j, x], w_recv.at[j, x], own_sem.at[j]).start()

    def wait_weights(j):
        for n, i in enumerate(X_DISTS):
            col = (x - i + NX) % NX
            remote(w_recv.at[j, col], w_recv.at[j, col], w_s.at[j, n], w_r.at[j, n], at_x(col)).wait_recv()
        pltpu.make_async_copy(w_send.at[j, x], w_recv.at[j, x], own_sem.at[j]).wait()

    def full_weights(j):
        wait_second(j)
        wait_weights(j)

        @pl.loop(0, NX)
        def _(c):
            for q in range(NZ):
                full[j, pl.ds(c * 2 * RANK, 2 * RANK), q * RANK : (q + 1) * RANK] = dot(
                    w_recv[j, c, q], sec[j, q, c]
                ).astype(BF16)

    def leaf_levels(j, rows_of):
        for l in range(4):
            leaf_c[j, l * RANK : (l + 1) * RANK] = dot(leaf_t[j, l], rows_of(l)).astype(BF16)
        a = jnp.concatenate([first_v[j, :, k].reshape(4 * RANK, RANK) for k in range(4)], axis=1)
        m_send[j] = dot(a, leaf_c[j]).astype(BF16).reshape(4, RANK, COLS)

    pair, odd = z // 2, z % 2
    near = [(z + 2 - odd) % NZ, (z + 5 - 2 * odd) % NZ, (z + 7 - odd) % NZ]
    side = 2 * odd - 1

    def send_mid(j):
        for t, plane in enumerate(near):
            s = (pair + t + 1) % 4
            start(remote(m_send.at[j, s], m_recv.at[j, z], m_s.at[j, t], m_r.at[j, z], at_z(plane)))
        start(remote(m_send.at[j, pair], m_recv.at[j, z], m_s.at[j, 3], m_r.at[j, z], at_z(other_z)))
        pltpu.make_async_copy(m_send.at[j, pair], m_recv.at[j, z], own_sem.at[3 + j]).start()

    def pass_mid(j):
        for n, i in enumerate((1, 2, 3)):
            plane = (z + side * i + NZ) % NZ
            here = m_recv.at[j, plane]
            remote(here, here, m_s.at[j, 4 + n], m_r.at[j, plane], at_z(plane)).wait_recv()
            start(remote(here, here, m_s.at[j, 4 + n], m_r.at[j, plane], at_z(other_z)))

    def wait_mid(j):
        for i in (1, 2, 3, 4):
            plane = (z - side * i + NZ) % NZ
            here = m_recv.at[j, plane]
            remote(here, here, m_s.at[j, 4], m_r.at[j, plane], at_z(plane)).wait_recv()
        pltpu.make_async_copy(m_send.at[j, pair], m_recv.at[j, z], own_sem.at[3 + j]).wait()

    def partial(j):
        for n, i in enumerate(X_DISTS + (0,)):
            col = (x + i) % NX
            a = full[j, pl.ds(pl.multiple_of(col * 2 * RANK, 2 * RANK), 2 * RANK)]
            p_send[j, col] = dot(a, m_recv[j].reshape(NZ * RANK, COLS)).astype(BF16)
            if i:
                start(remote(p_send.at[j, col], p_recv.at[j, n], p_s.at[j, n], p_r.at[j, n], at_x(col)))

    def halves(j):
        total = p_send[j, x].astype(F32)
        for n in range(3):
            here = p_recv.at[j, n]
            remote(here, here, p_s.at[j, n], p_r.at[j, n], at_x(x)).wait_recv()
            total += p_recv[j, n].astype(F32)
        half[j] = total.astype(BF16)

    send_second(0)
    send_second(1)
    outer_weights(0)
    outer_weights(1)
    outer_weights(2)
    loads[6].wait()
    for j in range(3):
        for l in range(4):
            leaf_t[j, l] = leaf_v[j, l].T
    loads[7].wait()
    loads[8].wait()
    for n, i in enumerate((1, 3, 2)):
        chip = ((y - i + NY) % NY) * 2 + core
        here = gath.at[:, chip]
        remote(here, here, ag_s.at[4 + n], ag_r.at[chip], partner).wait_recv()
        start(remote(here, here, ag_s.at[4 + n], ag_r.at[chip], partner))
    for i in (0, 1, 3, 2):
        chip = ((y - i + NY) % NY) * 2 + 1 - core
        here = gath.at[:, chip]
        remote(here, here, ag_s.at[0], ag_r.at[chip], partner).wait_recv()
    for j in range(2):
        leaf_levels(j, lambda l: gath[j, 2 * l : 2 * l + 2].reshape(2 * RANK, COLS))
        send_mid(j)
    full_weights(0)
    pass_mid(0)
    full_weights(1)
    wait_mid(0)
    partial(0)
    pass_mid(1)
    send_second(2)
    wait_mid(1)
    partial(1)
    halves(0)
    loads[9].wait()
    loads[10].wait()
    halves(1)
    for h in range(2):
        here = pl.ds(h * 4 * RANK, 4 * RANK)
        a = jnp.concatenate([outer_v[0, h], outer_v[1, h]], axis=1)
        b = jnp.concatenate([half[0, h * RANK : (h + 1) * RANK], half[1, h * RANK : (h + 1) * RANK]], axis=0)
        value = rhs_v[here].astype(F32) - dot(a, b)
        res[here] = value
        res_b[here] = value.astype(BF16)
    leaf_levels(2, lambda l: res_b[l * 2 * RANK : (l + 1) * 2 * RANK])
    send_mid(2)
    full_weights(2)
    pass_mid(2)
    wait_mid(2)
    partial(2)
    halves(2)
    for h in range(2):
        here = pl.ds(h * 4 * RANK, 4 * RANK)
        out[0, here] = (res[here] + dot(outer_v[2, h], half[2, h * RANK : (h + 1) * RANK])).astype(BF16)
    for copy in sends:
        copy.wait_send()


def on_device(*args):
    vmem = pltpu.VMEM
    dma = pltpu.SemaphoreType.DMA
    return pl.pallas_call(
        kernel,
        out_shape=jax.ShapeDtypeStruct((1, 1024, COLS), BF16),
        in_specs=[pl.BlockSpec(memory_space=pl.ANY)] * 8,
        out_specs=pl.BlockSpec(memory_space=pltpu.VMEM),
        scratch_shapes=[
            vmem((2, 8, RANK, COLS), BF16),
            vmem((3, 4, 2 * RANK, RANK), BF16),
            vmem((3, 4, RANK, 2 * RANK), BF16),
            vmem((3, 4, 4, RANK, RANK), BF16),
            vmem((3, 32, RANK, RANK), BF16),
            vmem((3, 2, NZ, RANK, RANK), BF16),
            vmem((3, 2, 4 * RANK, RANK), BF16),
            vmem((1024, COLS), BF16),
            vmem((3, NX, NZ, 2 * RANK, RANK), BF16),
            vmem((3, NX, NZ, 2 * RANK, RANK), BF16),
            vmem((3, NZ, NX, RANK, RANK), BF16),
            vmem((3, 8 * RANK, 8 * RANK), BF16),
            vmem((3, 4 * RANK, COLS), BF16),
            vmem((3, 4, RANK, COLS), BF16),
            vmem((3, NZ, RANK, COLS), BF16),
            vmem((3, NX, 2 * RANK, COLS), BF16),
            vmem((3, 3, 2 * RANK, COLS), BF16),
            vmem((3, 2 * RANK, COLS), BF16),
            vmem((1024, COLS), F32),
            vmem((1024, COLS), BF16),
            dma((14,)),
            dma((6,)),
            dma((7,)),
            dma((8,)),
            dma((3, 3)),
            dma((3, 3)),
            dma((3, 7)),
            dma((3, 7)),
            dma((3, 7)),
            dma((3, 8)),
            dma((3, 3)),
            dma((3, 3)),
        ],
        compiler_params=pltpu.CompilerParams(
            collective_id=0, has_side_effects=True, vmem_limit_bytes=67043328
        ),
    )(*args)


def solution(mesh):
    placed = (
        P(None, ("box", "row"), None),
        P("row", "box", None),
        P("row", None, "box", None, None),
        P("row", None, "box", None, None, None, None),
        P("row", None, "box", None, None, None),
        P("row", None, "box", None, None, None),
        P("row", None, "box", None, None, None, None),
        P("row", None, "box", None, None),
    )
    return jax.shard_map(on_device, mesh=mesh, in_specs=placed, out_specs=P("row", "box", None), check_vma=False)
```

time: 357 us -> 154 us (0.43)
  waiting for transfers between devices: 209 us -> 0 us
  Pallas kernels: 0 us -> 151 us
  local copies, waits for them, and re-layouts: 57 us -> 2.26 us
  starting transfers between devices: 28.2 us -> 0 us
  matrix products: 24.6 us -> 0 us
  blocking collectives: 18 us -> 0 us
  between operations: 13.5 us -> 0.01 us
  other arithmetic: 5.76 us -> 0 us
    all_to_all x5 -> x0, waiting for transfers between devices: 180 us -> none  [the longest x1 67.7 us: on_device(): lax.all_to_all(outer_w, 'box', 0, 0, axis_index_groups=along_x, tiled=True)]
    pallas_call x0 -> x1, Pallas kernels: none -> 151 us  [on_device(): pl.pallas_call(kernel, out_shape=jax.ShapeDtypeStruct((1, 1024, COLS), BF...]
    all_gather x1 -> x0, waiting for transfers between devices: 28.5 us -> none  [on_device(): gathered = lax.all_gather(solved, 'row', axis=1, tiled=True)]
    all_to_all x5 -> x0, starting transfers between devices: 28.2 us -> none  [the longest x2 9.88 us: middle(): lax.all_to_all(mid, 'box', 1, 1, axis_index_groups=along_z, tiled=True)]
    dot_general x8 -> x0, matrix products: 24.6 us -> none  [dot(): return jnp.einsum(spec, a, b, preferred_element_type=F32)]
    slice x7 -> x0, local copies, waits for them, and re-layouts: 20.2 us -> none  [the longest x6 17.7 us: middle(): full[js]]
    all_to_all x1 -> x0, blocking collectives: 18 us -> none  [middle(): lax.all_to_all(part, 'box', 1, 1, axis_index_groups=along_x, tiled=True)]
    convert_element_type x5 -> x0, local copies, waits for them, and re-layouts: 12.5 us -> none  [the longest x1 8.61 us: on_device(): outer_w = dot('jhqab,jqkbc->kjhaqc', fourth, third).astype(BF16)]
  transfers between devices with their start and end apart: 6 -> 0, of which waited for: 6 -> 0; matrix products, arithmetic and copies ran while one was open for 10% -> 0% of each run, Pallas kernels for 0% -> 0%
where the time goes in v2:
time: 154 us
  Pallas kernels  151 us (98%)
  local copies, waits for them, and re-layouts  2.26 us (1%)
    pallas_call x1, Pallas kernels, on_device(): pl.pallas_call(kernel, out_shape=jax.ShapeDtypeStruct((1, 1024, COLS), BF...  151 us

profile of v2, /device:TPU:16, one launch (start us, length us, event | category | flops | bytes accessed | tf_op | source)
XLA Modules:
  0.0 153.6 jit_solution(5877639772497170528)
XLA Ops:
  0.0 151.4 %shard_map.82 = bf16[1,1024,512]{2,1,0:T(8,128)(2,1)} custom-call(bf16[2,128,512]{2,1,0:T(8,128)(2,1)} %solved.1, bf16[1,1024,512]{2,1,0:T(8,128)(2,1)} %rhs.1, bf16[1,3,4,256,128]{4,3,2,1,0:T(8,128)(2,1)} %leaf.1, bf16[1,3,1,4,4,128,128]{6,5,4,3,2,1,0:T(8,128)(2,1)} %first.1, bf16[1,3,1,32,128,128]{5,4,3,2,1,0:T(8,128)(2,1)} %second.1, ...), custom_call_target="tpu_custom_call" | custom-call | tf_op jit(solution)/shard_map/pallas_call | solution.py:239
  151.4 2.3 %copy.10 = bf16[1,1024,512]{2,1,0:T(8,128)(2,1)} copy(bf16[1,1024,512]{2,1,0:T(8,128)(2,1)} %shard_map.82) | data formatting | bytes 2097152

commit v3 on v2

--- a/solution.py
+++ b/solution.py
@@ -14,6 +14,7 @@
 X_DISTS = (2, 1, 3)
 Z_DISTS = (4, 3, 5, 2, 6, 1, 7)
 RANK, COLS = 128, 512
+EARLY, LATE = 2, 4
 
 
 def dot(a, b):
@@ -23,9 +24,22 @@
 def kernel(
     solved, rhs, leaf, first, second, third, fourth, outer, out,
     gath, leaf_v, leaf_t, first_v, third_v, fourth_v, outer_v, rhs_v,
-    w_send, w_recv, sec, full, leaf_c, m_send, m_recv, p_send, p_recv, half, res, res_b,
-    load_sem, own_sem, ag_s, ag_r, w_s, w_r, sec_s, sec_r, m_s, m_r, p_s, p_r,
+    w_send, w_recv, sec, full, half, res, res_b, out_v,
+    m_send0, m_recv0, p_send0, p_recv0, m_send1, m_recv1, p_send1, p_recv1,
+    load_sem, own_sem, out_sem, ag_s, ag_r, w_s, w_r, sec_s, sec_r,
+    m_s0, m_r0, p_s0, p_r0, own0, m_s1, m_r1, p_s1, p_r1, own1,
 ):
+    early = (m_send0, m_recv0, p_send0, p_recv0, m_s0, m_r0, p_s0, p_r0, own0, EARLY, 0)
+    late = (m_send1, m_recv1, p_send1, p_recv1, m_s1, m_r1, p_s1, p_r1, own1, LATE, 2)
+
+    def unit(j, c):
+        *refs, chunks, base = late if j == 2 else early
+        return (*refs, (j - base) * chunks + c)
+
+    def cut(j, c):
+        width = COLS // (LATE if j == 2 else EARLY)
+        return slice(c * width, (c + 1) * width)
+
     row, box = lax.axis_index("row"), lax.axis_index("box")
     y, core = row // 2, row % 2
     z, x = box // NX, box % NX
@@ -84,8 +98,8 @@
         start(remote(solved, gath.at[:, row], ag_s.at[n], ag_r.at[row], at_y((y + i) % NY)))
     start(remote(solved, gath.at[:, row], ag_s.at[3], ag_r.at[row], partner))
 
-    def send_second(j):
-        for n, i in enumerate(Z_DISTS):
+    def send_second(j, begin=0, end=7):
+        for n, i in list(enumerate(Z_DISTS))[begin:end]:
             plane = (z + i) % NZ
             start(remote(second.at[0, j, 0, pl.ds(plane * NX, NX)], sec.at[j, z], sec_s.at[j, n], sec_r.at[j, n], at_z(plane)))
 
@@ -129,55 +143,83 @@
                     w_recv[j, c, q], sec[j, q, c]
                 ).astype(BF16)
 
-    def leaf_levels(j, rows_of):
-        for l in range(4):
-            leaf_c[j, l * RANK : (l + 1) * RANK] = dot(leaf_t[j, l], rows_of(l)).astype(BF16)
+    def leaf_levels(j, c, rows_of):
+        m_send, *_, u = unit(j, c)
+        coef = jnp.concatenate([dot(leaf_t[j, l], rows_of(l)).astype(BF16) for l in range(4)], axis=0)
         a = jnp.concatenate([first_v[j, :, k].reshape(4 * RANK, RANK) for k in range(4)], axis=1)
-        m_send[j] = dot(a, leaf_c[j]).astype(BF16).reshape(4, RANK, COLS)
+        m_send[u] = dot(a, coef).astype(BF16).reshape(4, RANK, -1)
 
     pair, odd = z // 2, z % 2
     near = [(z + 2 - odd) % NZ, (z + 5 - 2 * odd) % NZ, (z + 7 - odd) % NZ]
     side = 2 * odd - 1
 
-    def send_mid(j):
+    def own_mid(j, c):
+        m_send, m_recv, _, _, _, _, _, _, own, u = unit(j, c)
+        return pltpu.make_async_copy(m_send.at[u, pair], m_recv.at[u, z], own.at[u])
+
+    def send_mid(j, c):
+        m_send, m_recv, _, _, m_s, m_r, _, _, _, u = unit(j, c)
         for t, plane in enumerate(near):
             s = (pair + t + 1) % 4
-            start(remote(m_send.at[j, s], m_recv.at[j, z], m_s.at[j, t], m_r.at[j, z], at_z(plane)))
-        start(remote(m_send.at[j, pair], m_recv.at[j, z], m_s.at[j, 3], m_r.at[j, z], at_z(other_z)))
-        pltpu.make_async_copy(m_send.at[j, pair], m_recv.at[j, z], own_sem.at[3 + j]).start()
-
-    def pass_mid(j):
+            start(remote(m_send.at[u, s], m_recv.at[u, z], m_s.at[u, t], m_r.at[u, z], at_z(plane)))
+        start(remote(m_send.at[u, pair], m_recv.at[u, z], m_s.at[u, 3], m_r.at[u, z], at_z(other_z)))
+        own_mid(j, c).start()
+
+    def pass_mid(j, c):
+        _, m_recv, _, _, m_s, m_r, _, _, _, u = unit(j, c)
         for n, i in enumerate((1, 2, 3)):
             plane = (z + side * i + NZ) % NZ
-            here = m_recv.at[j, plane]
-            remote(here, here, m_s.at[j, 4 + n], m_r.at[j, plane], at_z(plane)).wait_recv()
-            start(remote(here, here, m_s.at[j, 4 + n], m_r.at[j, plane], at_z(other_z)))
-
-    def wait_mid(j):
+            here = m_recv.at[u, plane]
+            remote(here, here, m_s.at[u, 4 + n], m_r.at[u, plane], at_z(plane)).wait_recv()
+            start(remote(here, here, m_s.at[u, 4 + n], m_r.at[u, plane], at_z(other_z)))
+
+    def wait_mid(j, c):
+        _, m_recv, _, _, m_s, m_r, _, _, _, u = unit(j, c)
         for i in (1, 2, 3, 4):
             plane = (z - side * i + NZ) % NZ
-            here = m_recv.at[j, plane]
-            remote(here, here, m_s.at[j, 4], m_r.at[j, plane], at_z(plane)).wait_recv()
-        pltpu.make_async_copy(m_send.at[j, pair], m_recv.at[j, z], own_sem.at[3 + j]).wait()
-
-    def partial(j):
+            here = m_recv.at[u, plane]
+            remote(here, here, m_s.at[u, 4], m_r.at[u, plane], at_z(plane)).wait_recv()
+        own_mid(j, c).wait()
+
+    def partial(j, c):
+        _, m_recv, p_send, p_recv, _, _, p_s, p_r, _, u = unit(j, c)
         for n, i in enumerate(X_DISTS + (0,)):
             col = (x + i) % NX
             a = full[j, pl.ds(pl.multiple_of(col * 2 * RANK, 2 * RANK), 2 * RANK)]
-            p_send[j, col] = dot(a, m_recv[j].reshape(NZ * RANK, COLS)).astype(BF16)
+            p_send[u, col] = dot(a, m_recv[u].reshape(NZ * RANK, -1)).astype(BF16)
             if i:
-                start(remote(p_send.at[j, col], p_recv.at[j, n], p_s.at[j, n], p_r.at[j, n], at_x(col)))
-
-    def halves(j):
-        total = p_send[j, x].astype(F32)
+                start(remote(p_send.at[u, col], p_recv.at[u, n], p_s.at[u, n], p_r.at[u, n], at_x(col)))
+
+    def halves(j, c):
+        _, _, p_send, p_recv, _, _, p_s, p_r, _, u = unit(j, c)
+        total = p_send[u, x].astype(F32)
         for n in range(3):
-            here = p_recv.at[j, n]
-            remote(here, here, p_s.at[j, n], p_r.at[j, n], at_x(x)).wait_recv()
-            total += p_recv[j, n].astype(F32)
-        half[j] = total.astype(BF16)
+            here = p_recv.at[u, n]
+            remote(here, here, p_s.at[u, n], p_r.at[u, n], at_x(x)).wait_recv()
+            total += p_recv[u, n].astype(F32)
+        half[j, :, cut(j, c)] = total.astype(BF16)
+
+    def residual(c):
+        for h in range(2):
+            here = pl.ds(h * 4 * RANK, 4 * RANK)
+            part = slice(h * RANK, (h + 1) * RANK)
+            a = jnp.concatenate([outer_v[0, h], outer_v[1, h]], axis=1)
+            b = jnp.concatenate([half[0, part, cut(0, c)], half[1, part, cut(1, c)]], axis=0)
+            value = rhs_v[here, cut(0, c)].astype(F32) - dot(a, b)
+            res[here, cut(0, c)] = value
+            res_b[here, cut(0, c)] = value.astype(BF16)
+
+    def put(c):
+        return pltpu.make_async_copy(out_v.at[:, cut(2, c)], out.at[0, :, cut(2, c)], out_sem.at[c])
+
+    def finish(c):
+        for h in range(2):
+            here = pl.ds(h * 4 * RANK, 4 * RANK)
+            value = res[here, cut(2, c)] + dot(outer_v[2, h], half[2, h * RANK : (h + 1) * RANK, cut(2, c)])
+            out_v[here, cut(2, c)] = value.astype(BF16)
+        put(c).start()
 
     send_second(0)
-    send_second(1)
     outer_weights(0)
     outer_weights(1)
     outer_weights(2)
@@ -197,38 +239,55 @@
         here = gath.at[:, chip]
         remote(here, here, ag_s.at[0], ag_r.at[chip], partner).wait_recv()
     for j in range(2):
-        leaf_levels(j, lambda l: gath[j, 2 * l : 2 * l + 2].reshape(2 * RANK, COLS))
-        send_mid(j)
+        for c in range(EARLY):
+            leaf_levels(j, c, lambda l: gath[j, 2 * l : 2 * l + 2, :, cut(j, c)].reshape(2 * RANK, -1))
+            send_mid(j, c)
+    send_second(1, 0, 1)
     full_weights(0)
-    pass_mid(0)
+    units = [(j, c) for j in range(2) for c in range(EARLY)]
+    for n, (j, c) in enumerate(units):
+        pass_mid(j, c)
+        send_second(1, 1 + 6 * n // len(units), 1 + 6 * (n + 1) // len(units))
+    send_second(2)
+    for c in range(EARLY):
+        wait_mid(0, c)
+        partial(0, c)
     full_weights(1)
-    wait_mid(0)
-    partial(0)
-    pass_mid(1)
-    send_second(2)
-    wait_mid(1)
-    partial(1)
-    halves(0)
+    for c in range(EARLY):
+        wait_mid(1, c)
+        partial(1, c)
     loads[9].wait()
     loads[10].wait()
-    halves(1)
-    for h in range(2):
-        here = pl.ds(h * 4 * RANK, 4 * RANK)
-        a = jnp.concatenate([outer_v[0, h], outer_v[1, h]], axis=1)
-        b = jnp.concatenate([half[0, h * RANK : (h + 1) * RANK], half[1, h * RANK : (h + 1) * RANK]], axis=0)
-        value = rhs_v[here].astype(F32) - dot(a, b)
-        res[here] = value
-        res_b[here] = value.astype(BF16)
-    leaf_levels(2, lambda l: res_b[l * 2 * RANK : (l + 1) * 2 * RANK])
-    send_mid(2)
+
+    def start_late(c):
+        leaf_levels(2, c, lambda l: res_b[l * 2 * RANK : (l + 1) * 2 * RANK, cut(2, c)])
+        send_mid(2, c)
+
+    for c in range(EARLY):
+        halves(0, c)
+        halves(1, c)
+        residual(c)
+        if c == 0:
+            start_late(0)
+            start_late(1)
     full_weights(2)
-    pass_mid(2)
-    wait_mid(2)
-    partial(2)
-    halves(2)
-    for h in range(2):
-        here = pl.ds(h * 4 * RANK, 4 * RANK)
-        out[0, here] = (res[here] + dot(outer_v[2, h], half[2, h * RANK : (h + 1) * RANK])).astype(BF16)
+    for c in range(LATE):
+        pass_mid(2, c)
+        if c + 2 < LATE:
+            start_late(c + 2)
+        if c:
+            wait_mid(2, c - 1)
+            partial(2, c - 1)
+        if c > 1:
+            halves(2, c - 2)
+            finish(c - 2)
+    wait_mid(2, LATE - 1)
+    partial(2, LATE - 1)
+    for c in range(LATE - 2, LATE):
+        halves(2, c)
+        finish(c)
+    for c in range(LATE):
+        put(c).wait()
     for copy in sends:
         copy.wait_send()
 
@@ -236,11 +295,12 @@
 def on_device(*args):
     vmem = pltpu.VMEM
     dma = pltpu.SemaphoreType.DMA
+    groups = ((2 * EARLY, EARLY), (LATE, LATE))
     return pl.pallas_call(
         kernel,
         out_shape=jax.ShapeDtypeStruct((1, 1024, COLS), BF16),
         in_specs=[pl.BlockSpec(memory_space=pl.ANY)] * 8,
-        out_specs=pl.BlockSpec(memory_space=pltpu.VMEM),
+        out_specs=pl.BlockSpec(memory_space=pl.ANY),
         scratch_shapes=[
             vmem((2, 8, RANK, COLS), BF16),
             vmem((3, 4, 2 * RANK, RANK), BF16),
@@ -254,26 +314,32 @@
             vmem((3, NX, NZ, 2 * RANK, RANK), BF16),
             vmem((3, NZ, NX, RANK, RANK), BF16),
             vmem((3, 8 * RANK, 8 * RANK), BF16),
-            vmem((3, 4 * RANK, COLS), BF16),
-            vmem((3, 4, RANK, COLS), BF16),
-            vmem((3, NZ, RANK, COLS), BF16),
-            vmem((3, NX, 2 * RANK, COLS), BF16),
-            vmem((3, 3, 2 * RANK, COLS), BF16),
             vmem((3, 2 * RANK, COLS), BF16),
             vmem((1024, COLS), F32),
             vmem((1024, COLS), BF16),
+            vmem((1024, COLS), BF16),
+            *[ref for units, chunks in groups for ref in (
+                vmem((units, 4, RANK, COLS // chunks), BF16),
+                vmem((units, NZ, RANK, COLS // chunks), BF16),
+                vmem((units, NX, 2 * RANK, COLS // chunks), BF16),
+                vmem((units, 3, 2 * RANK, COLS // chunks), BF16),
+            )],
             dma((14,)),
-            dma((6,)),
+            dma((3,)),
+            dma((LATE,)),
             dma((7,)),
             dma((8,)),
             dma((3, 3)),
             dma((3, 3)),
             dma((3, 7)),
             dma((3, 7)),
-            dma((3, 7)),
-            dma((3, 8)),
-            dma((3, 3)),
-            dma((3, 3)),
+            *[ref for units, _ in groups for ref in (
+                dma((units, 7)),
+                dma((units, 8)),
+                dma((units, 3)),
+                dma((units, 3)),
+                dma((units,)),
+            )],
         ],
         compiler_params=pltpu.CompilerParams(
             collective_id=0, has_side_effects=True, vmem_limit_bytes=67043328

time: 154 us -> 140 us (0.909)
  Pallas kernels: 151 us -> 138 us
    pallas_call x1, Pallas kernels: 151 us -> 138 us  [on_device(): pl.pallas_call(kernel, out_shape=jax.ShapeDtypeStruct((1, 1024, COLS), BF...]
where the time goes in v3:
time: 140 us
  Pallas kernels  138 us (99%)
  local copies, waits for them, and re-layouts  2.26 us (2%)
    pallas_call x1, Pallas kernels, on_device(): pl.pallas_call(kernel, out_shape=jax.ShapeDtypeStruct((1, 1024, COLS), BF...  138 us

profile of v3, /device:TPU:16, one launch (start us, length us, event | category | flops | bytes accessed | tf_op | source)
XLA Modules:
  0.0 140.3 jit_solution(9827789511666644393)
XLA Ops:
  0.0 138.0 %shard_map.82 = bf16[1,1024,512]{2,1,0:T(8,128)(2,1)} custom-call(bf16[2,128,512]{2,1,0:T(8,128)(2,1)} %solved.1, bf16[1,1024,512]{2,1,0:T(8,128)(2,1)} %rhs.1, bf16[1,3,4,256,128]{4,3,2,1,0:T(8,128)(2,1)} %leaf.1, bf16[1,3,1,4,4,128,128]{6,5,4,3,2,1,0:T(8,128)(2,1)} %first.1, bf16[1,3,1,32,128,128]{5,4,3,2,1,0:T(8,128)(2,1)} %second.1, ...), custom_call_target="tpu_custom_call" | custom-call | tf_op jit(solution)/shard_map/pallas_call | solution.py:299
  138.0 2.3 %copy.10 = bf16[1,1024,512]{2,1,0:T(8,128)(2,1)} copy(bf16[1,1024,512]{2,1,0:T(8,128)(2,1)} %shard_map.82) | data formatting | bytes 2097152

commit v4 on v3

--- a/solution.py
+++ b/solution.py
@@ -24,9 +24,9 @@
 def kernel(
     solved, rhs, leaf, first, second, third, fourth, outer, out,
     gath, leaf_v, leaf_t, first_v, third_v, fourth_v, outer_v, rhs_v,
-    w_send, w_recv, sec, full, half, res, res_b, out_v,
+    w_send, w_recv, sec, full, half, res, res_b,
     m_send0, m_recv0, p_send0, p_recv0, m_send1, m_recv1, p_send1, p_recv1,
-    load_sem, own_sem, out_sem, ag_s, ag_r, w_s, w_r, sec_s, sec_r,
+    load_sem, own_sem, ag_s, ag_r, w_s, w_r, sec_s, sec_r,
     m_s0, m_r0, p_s0, p_r0, own0, m_s1, m_r1, p_s1, p_r1, own1,
 ):
     early = (m_send0, m_recv0, p_send0, p_recv0, m_s0, m_r0, p_s0, p_r0, own0, EARLY, 0)
@@ -79,35 +79,26 @@
         (solved, gath.at[:, row]),
         (outer.at[0], outer_v),
         (rhs.at[0], rhs_v),
-        (second.at[0, 0, 0, pl.ds(z * NX, NX)], sec.at[0, z]),
-        (second.at[0, 1, 0, pl.ds(z * NX, NX)], sec.at[1, z]),
-        (second.at[0, 2, 0, pl.ds(z * NX, NX)], sec.at[2, z]),
+        (second.at[0, :, 0, pl.ds(z * NX, NX)], sec.at[:, z]),
     ]
     loads = [pltpu.make_async_copy(src, dst, load_sem.at[i]) for i, (src, dst) in enumerate(loads)]
     for copy in loads:
         copy.start()
     pl.semaphore_wait(barrier, len(peers))
 
-    sends = []
-
-    def start(copy):
-        copy.start()
-        sends.append(copy)
-
     for n, i in enumerate((1, 3, 2)):
-        start(remote(solved, gath.at[:, row], ag_s.at[n], ag_r.at[row], at_y((y + i) % NY)))
-    start(remote(solved, gath.at[:, row], ag_s.at[3], ag_r.at[row], partner))
+        remote(solved, gath.at[:, row], ag_s, ag_r.at[n], at_y((y + i) % NY)).start()
+    remote(solved, gath.at[:, row], ag_s, ag_r.at[3], partner).start()
 
     def send_second(j, begin=0, end=7):
-        for n, i in list(enumerate(Z_DISTS))[begin:end]:
+        for i in Z_DISTS[begin:end]:
             plane = (z + i) % NZ
-            start(remote(second.at[0, j, 0, pl.ds(plane * NX, NX)], sec.at[j, z], sec_s.at[j, n], sec_r.at[j, n], at_z(plane)))
+            remote(second.at[0, j, 0, pl.ds(plane * NX, NX)], sec.at[j, z], sec_s, sec_r.at[j], at_z(plane)).start()
 
     def wait_second(j):
-        for n, i in enumerate(Z_DISTS):
-            plane = (z - i + NZ) % NZ
-            remote(sec.at[j, plane], sec.at[j, plane], sec_s.at[j, n], sec_r.at[j, n], at_z(plane)).wait_recv()
-        loads[11 + j].wait()
+        remote(sec.at[j, :7], sec.at[j, :7], sec_s, sec_r.at[j], partner).wait_recv()
+        if j == 0:
+            loads[11].wait()
 
     def outer_weights(j):
         loads[2 * j].wait()
@@ -121,15 +112,13 @@
             for k in range(NX):
                 w_send[j, k, q] = o[:, k * RANK : (k + 1) * RANK]
 
-        for n, i in enumerate(X_DISTS):
+        for i in X_DISTS:
             col = (x + i) % NX
-            start(remote(w_send.at[j, col], w_recv.at[j, x], w_s.at[j, n], w_r.at[j, n], at_x(col)))
+            remote(w_send.at[j, col], w_recv.at[j, x], w_s, w_r.at[j], at_x(col)).start()
         pltpu.make_async_copy(w_send.at[j, x], w_recv.at[j, x], own_sem.at[j]).start()
 
     def wait_weights(j):
-        for n, i in enumerate(X_DISTS):
-            col = (x - i + NX) % NX
-            remote(w_recv.at[j, col], w_recv.at[j, col], w_s.at[j, n], w_r.at[j, n], at_x(col)).wait_recv()
+        remote(w_recv.at[j, :3], w_recv.at[j, :3], w_s, w_r.at[j], partner).wait_recv()
         pltpu.make_async_copy(w_send.at[j, x], w_recv.at[j, x], own_sem.at[j]).wait()
 
     def full_weights(j):
@@ -159,26 +148,22 @@
 
     def send_mid(j, c):
         m_send, m_recv, _, _, m_s, m_r, _, _, _, u = unit(j, c)
-        for t, plane in enumerate(near):
+        for t, (plane, n) in enumerate(zip(near, (1 - odd, 2, odd))):
             s = (pair + t + 1) % 4
-            start(remote(m_send.at[u, s], m_recv.at[u, z], m_s.at[u, t], m_r.at[u, z], at_z(plane)))
-        start(remote(m_send.at[u, pair], m_recv.at[u, z], m_s.at[u, 3], m_r.at[u, z], at_z(other_z)))
+            remote(m_send.at[u, s], m_recv.at[u, z], m_s, m_r.at[u, n], at_z(plane)).start()
+        remote(m_send.at[u, pair], m_recv.at[u, z], m_s, m_r.at[u, 3], at_z(other_z)).start()
         own_mid(j, c).start()
 
     def pass_mid(j, c):
         _, m_recv, _, _, m_s, m_r, _, _, _, u = unit(j, c)
         for n, i in enumerate((1, 2, 3)):
-            plane = (z + side * i + NZ) % NZ
-            here = m_recv.at[u, plane]
-            remote(here, here, m_s.at[u, 4 + n], m_r.at[u, plane], at_z(plane)).wait_recv()
-            start(remote(here, here, m_s.at[u, 4 + n], m_r.at[u, plane], at_z(other_z)))
+            here = m_recv.at[u, (z + side * i + NZ) % NZ]
+            remote(here, here, m_s, m_r.at[u, n], partner).wait_recv()
+            remote(here, here, m_s, m_r.at[u, 3], at_z(other_z)).start()
 
     def wait_mid(j, c):
         _, m_recv, _, _, m_s, m_r, _, _, _, u = unit(j, c)
-        for i in (1, 2, 3, 4):
-            plane = (z - side * i + NZ) % NZ
-            here = m_recv.at[u, plane]
-            remote(here, here, m_s.at[u, 4], m_r.at[u, plane], at_z(plane)).wait_recv()
+        remote(m_recv.at[u, :4], m_recv.at[u, :4], m_s, m_r.at[u, 3], partner).wait_recv()
         own_mid(j, c).wait()
 
     def partial(j, c):
@@ -188,14 +173,13 @@
             a = full[j, pl.ds(pl.multiple_of(col * 2 * RANK, 2 * RANK), 2 * RANK)]
             p_send[u, col] = dot(a, m_recv[u].reshape(NZ * RANK, -1)).astype(BF16)
             if i:
-                start(remote(p_send.at[u, col], p_recv.at[u, n], p_s.at[u, n], p_r.at[u, n], at_x(col)))
+                remote(p_send.at[u, col], p_recv.at[u, n], p_s, p_r.at[u], at_x(col)).start()
 
     def halves(j, c):
         _, _, p_send, p_recv, _, _, p_s, p_r, _, u = unit(j, c)
+        remote(p_recv.at[u], p_recv.at[u], p_s, p_r.at[u], partner).wait_recv()
         total = p_send[u, x].astype(F32)
         for n in range(3):
-            here = p_recv.at[u, n]
-            remote(here, here, p_s.at[u, n], p_r.at[u, n], at_x(x)).wait_recv()
             total += p_recv[u, n].astype(F32)
         half[j, :, cut(j, c)] = total.astype(BF16)
 
@@ -209,15 +193,11 @@
             res[here, cut(0, c)] = value
             res_b[here, cut(0, c)] = value.astype(BF16)
 
-    def put(c):
-        return pltpu.make_async_copy(out_v.at[:, cut(2, c)], out.at[0, :, cut(2, c)], out_sem.at[c])
-
     def finish(c):
         for h in range(2):
             here = pl.ds(h * 4 * RANK, 4 * RANK)
             value = res[here, cut(2, c)] + dot(outer_v[2, h], half[2, h * RANK : (h + 1) * RANK, cut(2, c)])
-            out_v[here, cut(2, c)] = value.astype(BF16)
-        put(c).start()
+            out[0, here, cut(2, c)] = value.astype(BF16)
 
     send_second(0)
     outer_weights(0)
@@ -230,14 +210,10 @@
     loads[7].wait()
     loads[8].wait()
     for n, i in enumerate((1, 3, 2)):
-        chip = ((y - i + NY) % NY) * 2 + core
-        here = gath.at[:, chip]
-        remote(here, here, ag_s.at[4 + n], ag_r.at[chip], partner).wait_recv()
-        start(remote(here, here, ag_s.at[4 + n], ag_r.at[chip], partner))
-    for i in (0, 1, 3, 2):
-        chip = ((y - i + NY) % NY) * 2 + 1 - core
-        here = gath.at[:, chip]
-        remote(here, here, ag_s.at[0], ag_r.at[chip], partner).wait_recv()
+        here = gath.at[:, ((y - i + NY) % NY) * 2 + core]
+        remote(here, here, ag_s, ag_r.at[n], partner).wait_recv()
+        remote(here, here, ag_s, ag_r.at[3], partner).start()
+    remote(gath.at[:, :4], gath.at[:, :4], ag_s, ag_r.at[3], partner).wait_recv()
     for j in range(2):
         for c in range(EARLY):
             leaf_levels(j, c, lambda l: gath[j, 2 * l : 2 * l + 2, :, cut(j, c)].reshape(2 * RANK, -1))
@@ -270,26 +246,25 @@
         if c == 0:
             start_late(0)
             start_late(1)
-    full_weights(2)
     for c in range(LATE):
         pass_mid(2, c)
         if c + 2 < LATE:
             start_late(c + 2)
+        if c == 0:
+            full_weights(2)
         if c:
             wait_mid(2, c - 1)
             partial(2, c - 1)
-        if c > 1:
-            halves(2, c - 2)
-            finish(c - 2)
     wait_mid(2, LATE - 1)
     partial(2, LATE - 1)
-    for c in range(LATE - 2, LATE):
+    for c in range(LATE):
         halves(2, c)
         finish(c)
-    for c in range(LATE):
-        put(c).wait()
-    for copy in sends:
-        copy.wait_send()
+    for there, sem in (
+        (gath.at[:, :7], ag_s), (sec.at[:, :7], sec_s), (w_recv.at[:, :3], w_s),
+        (m_recv0.at[:, :7], m_s0), (m_recv1.at[:, :7], m_s1), (p_recv0, p_s0), (p_recv1, p_s1),
+    ):
+        remote(there, there, sem, sem, partner).wait_send()
 
 
 def on_device(*args):
@@ -298,9 +273,9 @@
     groups = ((2 * EARLY, EARLY), (LATE, LATE))
     return pl.pallas_call(
         kernel,
-        out_shape=jax.ShapeDtypeStruct((1, 1024, COLS), BF16),
+        out_shape=vmem((1, 1024, COLS), BF16),
         in_specs=[pl.BlockSpec(memory_space=pl.ANY)] * 8,
-        out_specs=pl.BlockSpec(memory_space=pl.ANY),
+        out_specs=pl.BlockSpec(memory_space=pltpu.VMEM),
         scratch_shapes=[
             vmem((2, 8, RANK, COLS), BF16),
             vmem((3, 4, 2 * RANK, RANK), BF16),
@@ -317,32 +292,26 @@
             vmem((3, 2 * RANK, COLS), BF16),
             vmem((1024, COLS), F32),
             vmem((1024, COLS), BF16),
-            vmem((1024, COLS), BF16),
             *[ref for units, chunks in groups for ref in (
                 vmem((units, 4, RANK, COLS // chunks), BF16),
                 vmem((units, NZ, RANK, COLS // chunks), BF16),
                 vmem((units, NX, 2 * RANK, COLS // chunks), BF16),
                 vmem((units, 3, 2 * RANK, COLS // chunks), BF16),
             )],
-            dma((14,)),
+            dma((12,)),
             dma((3,)),
-            dma((LATE,)),
-            dma((7,)),
-            dma((8,)),
-            dma((3, 3)),
-            dma((3, 3)),
-            dma((3, 7)),
-            dma((3, 7)),
+            dma(()),
+            dma((4,)),
+            dma(()),
+            dma((3,)),
+            dma(()),
+            dma((3,)),
             *[ref for units, _ in groups for ref in (
-                dma((units, 7)),
-                dma((units, 8)),
-                dma((units, 3)),
-                dma((units, 3)),
-                dma((units,)),
+                dma(()), dma((units, 4)), dma(()), dma((units,)), dma((units,)),
             )],
         ],
         compiler_params=pltpu.CompilerParams(
-            collective_id=0, has_side_effects=True, vmem_limit_bytes=67043328
+            collective_id=0, has_side_effects=True, vmem_limit_bytes=60 << 20
         ),
     )(*args)
 

time: 140 us -> 136 us (0.971)
  Pallas kernels: 138 us -> 135 us
    pallas_call x1, Pallas kernels: 138 us -> 135 us  [on_device(): pl.pallas_call(kernel, out_shape=vmem((1, 1024, COLS), BF16), in_specs=[p...]
where the time goes in v4:
time: 136 us
  Pallas kernels  135 us (99%)
    pallas_call x1, Pallas kernels, on_device(): pl.pallas_call(kernel, out_shape=vmem((1, 1024, COLS), BF16), in_specs=[p...  135 us

profile of v4, /device:TPU:16, one launch (start us, length us, event | category | flops | bytes accessed | tf_op | source)
XLA Modules:
  0.0 136.4 jit_solution(5970476247569983061)
XLA Ops:
  0.0 135.4 %shard_map.82 = bf16[1,1024,512]{2,1,0:T(8,128)(2,1)S(1)} custom-call(bf16[2,128,512]{2,1,0:T(8,128)(2,1)} %solved.1, bf16[1,1024,512]{2,1,0:T(8,128)(2,1)} %rhs.1, bf16[1,3,4,256,128]{4,3,2,1,0:T(8,128)(2,1)} %leaf.1, bf16[1,3,1,4,4,128,128]{6,5,4,3,2,1,0:T(8,128)(2,1)} %first.1, bf16[1,3,1,32,128,128]{5,4,3,2,1,0:T(8,128)(2,1)} %second.1, ...), custom_call_target="tpu_custom_call" | custom-call | tf_op jit(solution)/shard_map/pallas_call | solution.py:274
  135.4 1.0 copy.10

commit v5 on v4

--- a/solution.py
+++ b/solution.py
@@ -12,7 +12,7 @@
 MESH = pl.DeviceIdType.MESH
 NX, NZ, NY = 4, 8, 4
 X_DISTS = (2, 1, 3)
-Z_DISTS = (4, 3, 5, 2, 6, 1, 7)
+Z_DISTS = (1, 7, 2, 6, 3, 5, 4)
 RANK, COLS = 128, 512
 EARLY, LATE = 2, 4
 
@@ -27,10 +27,10 @@
     w_send, w_recv, sec, full, half, res, res_b,
     m_send0, m_recv0, p_send0, p_recv0, m_send1, m_recv1, p_send1, p_recv1,
     load_sem, own_sem, ag_s, ag_r, w_s, w_r, sec_s, sec_r,
-    m_s0, m_r0, p_s0, p_r0, own0, m_s1, m_r1, p_s1, p_r1, own1,
+    m_s0, m_r0, p_s0, p_r0, m_s1, m_r1, p_s1, p_r1,
 ):
-    early = (m_send0, m_recv0, p_send0, p_recv0, m_s0, m_r0, p_s0, p_r0, own0, EARLY, 0)
-    late = (m_send1, m_recv1, p_send1, p_recv1, m_s1, m_r1, p_s1, p_r1, own1, LATE, 2)
+    early = (m_send0, m_recv0, p_send0, p_recv0, m_s0, m_r0, p_s0, p_r0, EARLY, 0)
+    late = (m_send1, m_recv1, p_send1, p_recv1, m_s1, m_r1, p_s1, p_r1, LATE, 2)
 
     def unit(j, c):
         *refs, chunks, base = late if j == 2 else early
@@ -142,32 +142,27 @@
     near = [(z + 2 - odd) % NZ, (z + 5 - 2 * odd) % NZ, (z + 7 - odd) % NZ]
     side = 2 * odd - 1
 
-    def own_mid(j, c):
-        m_send, m_recv, _, _, _, _, _, _, own, u = unit(j, c)
-        return pltpu.make_async_copy(m_send.at[u, pair], m_recv.at[u, z], own.at[u])
-
     def send_mid(j, c):
-        m_send, m_recv, _, _, m_s, m_r, _, _, _, u = unit(j, c)
+        m_send, m_recv, _, _, m_s, m_r, _, _, u = unit(j, c)
         for t, (plane, n) in enumerate(zip(near, (1 - odd, 2, odd))):
             s = (pair + t + 1) % 4
             remote(m_send.at[u, s], m_recv.at[u, z], m_s, m_r.at[u, n], at_z(plane)).start()
         remote(m_send.at[u, pair], m_recv.at[u, z], m_s, m_r.at[u, 3], at_z(other_z)).start()
-        own_mid(j, c).start()
+        m_recv[u, z] = m_send[u, pair]
 
     def pass_mid(j, c):
-        _, m_recv, _, _, m_s, m_r, _, _, _, u = unit(j, c)
+        _, m_recv, _, _, m_s, m_r, _, _, u = unit(j, c)
         for n, i in enumerate((1, 2, 3)):
             here = m_recv.at[u, (z + side * i + NZ) % NZ]
             remote(here, here, m_s, m_r.at[u, n], partner).wait_recv()
             remote(here, here, m_s, m_r.at[u, 3], at_z(other_z)).start()
 
     def wait_mid(j, c):
-        _, m_recv, _, _, m_s, m_r, _, _, _, u = unit(j, c)
+        _, m_recv, _, _, m_s, m_r, _, _, u = unit(j, c)
         remote(m_recv.at[u, :4], m_recv.at[u, :4], m_s, m_r.at[u, 3], partner).wait_recv()
-        own_mid(j, c).wait()
 
     def partial(j, c):
-        _, m_recv, p_send, p_recv, _, _, p_s, p_r, _, u = unit(j, c)
+        _, m_recv, p_send, p_recv, _, _, p_s, p_r, u = unit(j, c)
         for n, i in enumerate(X_DISTS + (0,)):
             col = (x + i) % NX
             a = full[j, pl.ds(pl.multiple_of(col * 2 * RANK, 2 * RANK), 2 * RANK)]
@@ -176,7 +171,7 @@
                 remote(p_send.at[u, col], p_recv.at[u, n], p_s, p_r.at[u], at_x(col)).start()
 
     def halves(j, c):
-        _, _, p_send, p_recv, _, _, p_s, p_r, _, u = unit(j, c)
+        _, _, p_send, p_recv, _, _, p_s, p_r, u = unit(j, c)
         remote(p_recv.at[u], p_recv.at[u], p_s, p_r.at[u], partner).wait_recv()
         total = p_send[u, x].astype(F32)
         for n in range(3):
@@ -307,7 +302,7 @@
             dma(()),
             dma((3,)),
             *[ref for units, _ in groups for ref in (
-                dma(()), dma((units, 4)), dma(()), dma((units,)), dma((units,)),
+                dma(()), dma((units, 4)), dma(()), dma((units,)),
             )],
         ],
         compiler_params=pltpu.CompilerParams(

time: 136 us -> 136 us (level)
  no operation moved by 1% of the time
where the time goes in v5:
time: 136 us
  Pallas kernels  135 us (99%)
    pallas_call x1, Pallas kernels, on_device(): pl.pallas_call(kernel, out_shape=vmem((1, 1024, COLS), BF16), in_specs=[p...  135 us

profile of v5, /device:TPU:16, one launch (start us, length us, event | category | flops | bytes accessed | tf_op | source)
XLA Modules:
  0.0 136.1 jit_solution(9135747940261655370)
XLA Ops:
  0.0 135.1 %shard_map.82 = bf16[1,1024,512]{2,1,0:T(8,128)(2,1)S(1)} custom-call(bf16[2,128,512]{2,1,0:T(8,128)(2,1)} %solved.1, bf16[1,1024,512]{2,1,0:T(8,128)(2,1)} %rhs.1, bf16[1,3,4,256,128]{4,3,2,1,0:T(8,128)(2,1)} %leaf.1, bf16[1,3,1,4,4,128,128]{6,5,4,3,2,1,0:T(8,128)(2,1)} %first.1, bf16[1,3,1,32,128,128]{5,4,3,2,1,0:T(8,128)(2,1)} %second.1, ...), custom_call_target="tpu_custom_call" | custom-call | tf_op jit(solution)/shard_map/pallas_call | solution.py:269
  135.1 1.0 copy.10
